TPU v7x, 256 devices: a whole 4x4x8 slice. The times are simulated.
256 devices in a mesh: dp: 4 (over x), depth: 2 (over y_hi), tensor: 32 (over y_lo, z, core).
Axes of the slice: x: 4, y: 4 (y_hi: 2, y_lo: 2; y = y_hi * 2 + y_lo), z: 8, core: 2. Of those that a mesh axis runs over, the one named last changes fastest.
Arguments:
- text: bfloat16 [512, 8192], P(('dp', 'tensor')), may hold values from -6 to 6
- vision: bfloat16 [1024, 8192], P(('dp', 'depth'), 'tensor'), may hold values from -6 to 6
- query_weight: bfloat16 [2, 8192, 8192], P('depth', None, 'tensor'), may hold values from -0.0625 to 0.0625
- key_weight: bfloat16 [2, 8192, 1024], P('depth', 'tensor'), may hold values from -0.0625 to 0.0625
- value_weight: bfloat16 [2, 8192, 1024], P('depth', 'tensor'), may hold values from -0.0625 to 0.0625
- out_weight: bfloat16 [2, 8192, 8192], P('depth', 'tensor'), may hold values from -0.25 to 0.25
- gate: float32 [2], P('depth'), may hold values from 0.5 to 1.5
- cotangent: bfloat16 [512, 8192], P(('dp', 'tensor')), may hold values from -0.75 to 0.75
- tile_table: int32 [4, 8, 4], P('dp'), may hold values 0 or 1
- vision_tiles: int32 [4], P('dp'), may hold values from 1 to 4
- text_lengths: int32 [4], P('dp'), may hold values from 64 to 128
Outputs:
- hidden_states: bfloat16 [2, 512, 8192], P('depth', ('dp', 'tensor'))
- text_grads: bfloat16 [2, 512, 8192], P('depth', ('dp', 'tensor'))
- vision_grad: float32 [1024, 8192], P(('dp', 'depth'), 'tensor')
- key_weight_grad: float32 [2, 8192, 1024], P('depth', 'tensor', 'dp')
- value_weight_grad: float32 [2, 8192, 1024], P('depth', 'tensor', 'dp')
All inputs are finite; a program needn't handle non-finite values. No bound on the sum of `tile_table` on one device may be relied on, other than what follows from the above.
Results may differ from a plain program's by a relative error of at most 0.034.
Values may be sent and summed in bfloat16 or wider, within the bound.
No kernel may reach another device: no remote copies, remote signals or barrier semaphores. Data moves between devices by JAX's collectives and lax.ppermute only.
A program may use at most 128 MiB of HBM per device.

v0:
```python
import math
import jax
import jax.numpy as jnp
from jax import lax
from jax.sharding import PartitionSpec as P

HD = 128
QGROUP = 8
SEQ = 128
TBLK = 16
TILES = 4
TILE_ROWS = 64
VIS = 256


def shifted(value, axis, steps):
    count = lax.axis_size(axis)
    first, last = (max(0, -steps), min(count, count - steps))
    return lax.ppermute(value, axis, [(source, source + steps) for source in range(first, last)])


def normalize(values, epsilon):
    return values * lax.rsqrt(jnp.mean(values * values, axis=-1, keepdims=True) + epsilon)


def norm_back(values, upstream, epsilon):
    inv_rms = lax.rsqrt(jnp.mean(values * values, axis=-1, keepdims=True) + epsilon)
    normed = values * inv_rms
    return inv_rms * (upstream - normed * jnp.mean(upstream * normed, axis=-1, keepdims=True))


def allowed_mask(table, tile_count, text_count):
    tile_ok = jnp.arange(TILES, dtype=jnp.int32) < tile_count
    block_ok = (table > 0) & tile_ok[None, :]
    full_mask = jnp.broadcast_to(
        block_ok[:, None, :, None], (SEQ // TBLK, TBLK, TILES, TILE_ROWS)
    ).reshape(SEQ, VIS)
    row_ok = jnp.arange(SEQ, dtype=jnp.int32) < text_count
    return full_mask & row_ok[:, None]


def token_rows(shard, transform):
    return transform(lax.all_gather(shard, "tensor", axis=0, tiled=True), jnp.int32(0))


def token_sums(term, shard_rows):
    return lax.psum_scatter(
        term(jnp.int32(0), shard_rows * lax.axis_size("tensor")).astype(jnp.bfloat16),
        "tensor",
        scatter_dimension=0,
        tiled=True,
    ).astype(jnp.float32)


def kv_totals(keys_part, values_part):
    return lax.psum((keys_part, values_part), "tensor")


def per_device(
    text,
    vision,
    query_weight,
    key_weight,
    value_weight,
    out_weight,
    gate,
    cotangent,
    tile_table,
    vision_tiles,
    text_lengths,
):
    layers = lax.axis_size("depth")
    section_index = lax.axis_index("depth")
    tensor_index = lax.axis_index("tensor")
    w_query = query_weight[0]
    w_key = key_weight[0]
    w_value = value_weight[0]
    w_out = out_weight[0]
    gate_value = jnp.tanh(gate[0])
    local_width = w_query.shape[1]
    local_heads = local_width // HD
    kv_width = w_key.shape[1]
    kv_heads = kv_width // HD
    shard_rows = text.shape[0]
    inv_sqrt = 1.0 / math.sqrt(HD)
    kv_group = tensor_index * local_heads // QGROUP
    allowed = allowed_mask(tile_table[0], vision_tiles[0], text_lengths[0])
    row_live = jnp.any(allowed, axis=-1).astype(jnp.float32)
    vis_full = lax.all_gather(vision, "depth", axis=0, tiled=True)
    keys_part = jnp.dot(vis_full, w_key, preferred_element_type=jnp.float32)
    values_part = jnp.dot(vis_full, w_value, preferred_element_type=jnp.float32)
    keys_pre, values_pre = kv_totals(keys_part, values_part)
    keys_cast = (
        normalize(keys_pre.reshape(VIS, kv_heads, HD), 1e-06)
        .astype(jnp.bfloat16)
        .reshape(VIS, kv_width)
    )
    values_cast = values_pre.astype(jnp.bfloat16)
    key_group = lax.dynamic_slice_in_dim(keys_cast, kv_group * HD, HD, 1)
    value_group = lax.dynamic_slice_in_dim(values_cast, kv_group * HD, HD, 1)
    current = text
    for layer_at in range(layers):

        def project(rows_in, offset):
            normed = normalize(rows_in.astype(jnp.float32), 1e-05).astype(jnp.bfloat16)
            return jnp.dot(normed, w_query, preferred_element_type=jnp.float32)

        layer_queries = token_rows(current, project).reshape(SEQ, local_heads, HD)
        layer_query_cast = normalize(layer_queries, 1e-06).astype(jnp.bfloat16)
        scores = (
            jnp.einsum(
                "shd,vd->hsv", layer_query_cast, key_group, preferred_element_type=jnp.float32
            )
            * inv_sqrt
        )
        expd = jnp.where(allowed[None], jnp.exp(scores), 0.0)
        layer_probs = expd / (
            jnp.sum(expd, axis=-1, keepdims=True) + (1.0 - row_live)[None, :, None]
        )
        layer_probs_cast = layer_probs.astype(jnp.bfloat16)
        mixed = jnp.einsum(
            "hsv,vd->shd", layer_probs_cast, value_group, preferred_element_type=jnp.float32
        )
        mixed_cast = mixed.astype(jnp.bfloat16).reshape(SEQ, local_width)

        def out_term(offset, number):
            return jnp.dot(mixed_cast, w_out, preferred_element_type=jnp.float32)

        attended = token_sums(out_term, shard_rows)
        outputs = (current.astype(jnp.float32) + gate_value * attended).astype(jnp.bfloat16)
        outputs, kept = (outputs, (layer_queries, layer_query_cast, layer_probs, layer_probs_cast))
        chosen = section_index == layer_at
        if layer_at == 0:
            saved_in, saved_out, saved_kept = (current, outputs, kept)
        else:
            saved_in = jnp.where(chosen, current, saved_in)
            saved_out = jnp.where(chosen, outputs, saved_out)
            saved_kept = jax.tree.map(
                lambda fresh, older: jnp.where(chosen, fresh, older), kept, saved_kept
            )
        if layer_at + 1 < layers:
            current = shifted(outputs, "depth", 1)
    upstream = cotangent
    for layer_at in reversed(range(layers)):
        queries, query_cast, probs, probs_cast = saved_kept
        scaled = (gate_value * upstream.astype(jnp.float32)).astype(jnp.bfloat16)

        def back_project(rows_in, offset):
            return jnp.einsum("sd,kd->sk", rows_in, w_out, preferred_element_type=jnp.float32)

        dmixed = token_rows(scaled, back_project).astype(jnp.bfloat16).reshape(SEQ, local_heads, HD)
        dprobs = jnp.einsum("shd,vd->hsv", dmixed, value_group, preferred_element_type=jnp.float32)
        layer_dvalues = jnp.einsum(
            "hsv,shd->vd", probs_cast, dmixed, preferred_element_type=jnp.float32
        )
        dscores = (
            probs * (dprobs - jnp.sum(probs * dprobs, axis=-1, keepdims=True)) * inv_sqrt
        ).astype(jnp.bfloat16)
        dquery_hat = jnp.einsum(
            "hsv,vd->shd", dscores, key_group, preferred_element_type=jnp.float32
        )
        layer_dkeys_hat = jnp.einsum(
            "hsv,shd->vd", dscores, query_cast, preferred_element_type=jnp.float32
        )
        dquery = (
            norm_back(queries, dquery_hat, 1e-06).astype(jnp.bfloat16).reshape(SEQ, local_width)
        )

        def in_term(offset, number):
            return jnp.einsum("sk,dk->sd", dquery, w_query, preferred_element_type=jnp.float32)

        dnormed = token_sums(in_term, shard_rows)
        dinputs = (
            upstream.astype(jnp.float32) + norm_back(saved_in.astype(jnp.float32), dnormed, 1e-05)
        ).astype(jnp.bfloat16)
        dinputs, kv_grads = (dinputs, (layer_dkeys_hat, layer_dvalues))
        chosen = section_index == layer_at
        if layer_at == layers - 1:
            saved_grad, saved_kv = (dinputs, kv_grads)
        else:
            saved_grad = jnp.where(chosen, dinputs, saved_grad)
            saved_kv = jax.tree.map(
                lambda fresh, older: jnp.where(chosen, fresh, older), kv_grads, saved_kv
            )
        if layer_at > 0:
            upstream = shifted(dinputs, "depth", -1)
    dkeys_hat, dvalues = saved_kv
    one_hot = (jnp.arange(kv_heads, dtype=jnp.int32) == kv_group).astype(jnp.float32)
    dkeys_full = (dkeys_hat[:, None, :] * one_hot[None, :, None]).reshape(VIS, kv_width)
    dvalues_full = (dvalues[:, None, :] * one_hot[None, :, None]).reshape(VIS, kv_width)
    dkeys_total, dvalues_total = kv_totals(dkeys_full, dvalues_full)
    dkeys_cast = (
        norm_back(
            keys_pre.reshape(VIS, kv_heads, HD), dkeys_total.reshape(VIS, kv_heads, HD), 1e-06
        )
        .astype(jnp.bfloat16)
        .reshape(VIS, kv_width)
    )
    dvalues_cast = dvalues_total.astype(jnp.bfloat16)
    dvision_part = jnp.einsum(
        "vc,dc->vd", dkeys_cast, w_key, preferred_element_type=jnp.float32
    ) + jnp.einsum("vc,dc->vd", dvalues_cast, w_value, preferred_element_type=jnp.float32)
    dvision = lax.psum_scatter(dvision_part, "depth", scatter_dimension=0, tiled=True)
    dkey_part = jnp.einsum("vd,vc->dc", vis_full, dkeys_cast, preferred_element_type=jnp.float32)
    dvalue_part = jnp.einsum(
        "vd,vc->dc", vis_full, dvalues_cast, preferred_element_type=jnp.float32
    )
    dkey_grad, dvalue_grad = (
        lax.psum_scatter(dkey_part, "dp", scatter_dimension=1, tiled=True),
        lax.psum_scatter(dvalue_part, "dp", scatter_dimension=1, tiled=True),
    )
    return (saved_out[None], saved_grad[None], dvision, dkey_grad[None], dvalue_grad[None])


def solution(mesh):
    in_specs = (
        P(("dp", "tensor"), None),
        P(("dp", "depth"), "tensor"),
        P("depth", None, "tensor"),
        P("depth", "tensor", None),
        P("depth", "tensor", None),
        P("depth", "tensor", None),
        P("depth"),
        P(("dp", "tensor"), None),
        P("dp", None, None),
        P("dp"),
        P("dp"),
    )
    out_specs = (
        P("depth", ("dp", "tensor"), None),
        P("depth", ("dp", "tensor"), None),
        P(("dp", "depth"), "tensor"),
        P("depth", "tensor", "dp"),
        P("depth", "tensor", "dp"),
    )
    return jax.shard_map(
        per_device, mesh=mesh, in_specs=in_specs, out_specs=out_specs, check_vma=False
    )
```

profile of v0, /device:TPU:1, one launch (start us, length us, event | category | flops | bytes accessed | tf_op | source)
XLA Modules:
  0.0 1562.4 jit_solution(4551209075161023634)
XLA Ops:
  7.2 6.5 all_gather.15
  13.7 1.3 fusion.51
  15.8 6.5 copy.96
  24.4 2.5 and_reduce_fusion
  27.3 118.3 %all-reduce.22 = bf16[256,1024]{1,0:T(8,128)(2,1)} all-reduce(f32[256,1024]{1,0:T(8,128)S(1)} %fusion.54), channel_id=1, replica_groups=mesh['dp'=4,'depth'=2,'tensor'=32] {'tensor'}, use_global_device_ids=true, to_apply=%region_0.1 | all-reduce | flops 262144 | bytes 1572864 | tf_op jit(solution)/shard_map/psum | solution.py:56
  145.6 98.3 %all-reduce.13.cloned.1.call-done = f32[256,1024]{1,0:T(8,128)} async-done(((f32[256,1024]{1,0:T(8,128)}), f32[256,1024]{1,0:T(8,128)}) %all-reduce.13.cloned.1.call-update) | async-done | bytes 1048592 | tf_op jit(solution)/shard_map/psum | solution.py:56
  243.9 1.5 copy.99
  246.2 1.0 copy-done.5
  247.2 1.0 bitcast_multiply_fusion.3
  248.2 61.3 %all-gather.9.cloned.1.call-done = bf16[32,4,8192]{2,1,0:T(4,128)(2,1)} async-done(((bf16[1,4,8192]{2,1,0:T(4,128)(2,1)}), bf16[32,4,8192]{2,1,0:T(4,128)(2,1)}) %all-gather.9.cloned.1.call-update) | async-done | bytes 2097168 | tf_op jit(solution)/shard_map/all_gather | solution.py:43
  309.5 4.3 reshape.252
  313.8 2.7 multiply_reduce_fusion.1
  317.3 3.7 multiply_reduce_fusion.10
  321.1 1.1 fusion.107
  322.2 1.1 convolution_convert_fusion.5
  323.3 2.1 convolution_convert_fusion.3
  328.2 224.7 %all-reduce.17.cloned.1.call-done = bf16[128,8192]{1,0:T(8,128)(2,1)} async-done(((bf16[128,8192]{1,0:T(8,128)(2,1)}), bf16[128,8192]{1,0:T(8,128)(2,1)}) %all-reduce.17.cloned.1.call-update) | async-done | bytes 2097168
  552.9 1.0 add_convert_fusion.1
  553.9 4.3 collective-permute-start
  558.3 1.3 collective-permute-done
  560.5 58.4 %all-gather.13.cloned.1.call-done = bf16[32,4,8192]{2,1,0:T(4,128)(2,1)} async-done(((bf16[1,4,8192]{2,1,0:T(4,128)(2,1)}), bf16[32,4,8192]{2,1,0:T(4,128)(2,1)}) %all-gather.13.cloned.1.call-update) | async-done | bytes 2097168 | tf_op jit(solution)/shard_map/all_gather | solution.py:43
  618.8 4.0 reshape.249
  622.8 4.4 fusion.43
  627.1 1.7 convolution_bitcast_fusion.3
  628.9 56.7 %all-gather.11.cloned.1.call-done = bf16[32,4,8192]{2,1,0:T(4,128)(2,1)} async-done(((bf16[1,4,8192]{2,1,0:T(4,128)(2,1)}), bf16[32,4,8192]{2,1,0:T(4,128)(2,1)}) %all-gather.11.cloned.1.call-update) | async-done | bytes 2097168 | tf_op jit(solution)/shard_map/all_gather | solution.py:43
  685.5 4.3 reshape.253
  689.9 2.7 multiply_reduce_fusion
  693.3 3.6 multiply_reduce_fusion.9
  697.0 1.1 fusion.108
  698.2 0.8 broadcast_select_fusion.1
  698.9 1.5 multiply_reduce_fusion.7
  700.5 5.1 convolution_convert_fusion.1
  705.9 226.9 %all-reduce.19.cloned.1.call-done = bf16[128,8192]{1,0:T(8,128)(2,1)} async-done(((bf16[128,8192]{1,0:T(8,128)(2,1)}), bf16[128,8192]{1,0:T(8,128)(2,1)}) %all-reduce.19.cloned.1.call-update) | async-done | bytes 2097168
  932.8 1.2 fusion.71
  934.0 1.0 fusion.69
  935.0 1.3 collective-permute-start.1
  936.3 5.2 collective-permute-done.1
  942.4 2.1 convolution_bitcast_fusion.6
  944.5 0.8 convolution_bitcast_fusion.4
  945.3 59.2 %all-gather.15.cloned.1.call-done = bf16[32,4,8192]{2,1,0:T(4,128)(2,1)} async-done(((bf16[1,4,8192]{2,1,0:T(4,128)(2,1)}), bf16[32,4,8192]{2,1,0:T(4,128)(2,1)}) %all-gather.15.cloned.1.call-update) | async-done | bytes 2097168 | tf_op jit(solution)/shard_map/all_gather | solution.py:43
  1004.5 4.0 reshape.251
  1008.5 4.4 fusion.40
  1012.9 1.7 convolution_bitcast_fusion.2
  1014.8 1.5 fusion.38
  1016.4 1.8 bitcast_multiply_fusion
  1018.3 113.1 %all-reduce.23 = bf16[256,1024]{1,0:T(8,128)(2,1)S(1)} all-reduce(f32[256,1024]{1,0:T(8,128)} %get-tuple-element.29), channel_id=1, replica_groups=mesh['dp'=4,'depth'=2,'tensor'=32] {'tensor'}, use_global_device_ids=true, to_apply=%region_24.25 | all-reduce | flops 262144 | bytes 1572864 | tf_op jit(solution)/shard_map/psum | solution.py:56
  1131.4 1.3 convolution_bitcast_fusion
  1132.8 109.7 %all-reduce.15.cloned.1.call-done = f32[256,1024]{1,0:T(8,128)} async-done(((f32[256,1024]{1,0:T(8,128)}), f32[256,1024]{1,0:T(8,128)}) %all-reduce.15.cloned.1.call-update) | async-done | bytes 1048592 | tf_op jit(solution)/shard_map/psum | solution.py:56
  1242.5 1.6 copy.102
  1244.1 1.5 multiply_reduce_fusion.2
  1246.8 1.3 convolution_bitcast_fusion.1
  1248.4 1.0 convolution_convert_fusion.4
  1249.4 4.3 convolution_convert_fusion.2
  1253.7 1.5 multiply_reduce_fusion.6
  1255.3 5.0 convolution_convert_fusion
  1261.4 1.1 convolution_add_fusion
  1262.4 5.8 reduce-scatter.8.cloned.1.call-done
  1268.3 1.8 copy.79
  1270.0 26.7 %reduce-scatter.6.cloned.1.call-done = f32[256,256]{0,1:T(8,128)} async-done(((f32[256,1024]{0,1:T(8,128)}), f32[256,256]{0,1:T(8,128)}) %reduce-scatter.6.cloned.1.call-update) | async-done | bytes 262160 | tf_op jit(solution)/shard_map/reduce_scatter | solution.py:209
  1296.7 1.8 copy.78
  1298.5 237.2 %all-reduce.21.cloned.1.call-done = (bf16[128,8192]{1,0:T(8,128)(2,1)}, bf16[128,8192]{1,0:T(8,128)(2,1)}) async-done(((bf16[128,8192]{1,0:T(8,128)(2,1)}, bf16[128,8192]{1,0:T(8,128)(2,1)}), (bf16[128,8192]{1,0:T(8,128)(2,1)}, bf16[128,8192]{1,0:T(8,128)(2,1)})) %all-reduce.21.cloned.1.call-update) | async-done | bytes 4194320
  1535.7 1.2 fusion.75
  1536.9 1.8 fusion.84
  1538.8 16.8 %reduce-scatter.4.cloned.1.call-done = f32[128,256]{1,0:T(8,128)} async-done(((f32[256,256]{1,0:T(8,128)}), f32[128,256]{1,0:T(8,128)}) %reduce-scatter.4.cloned.1.call-update) | async-done | bytes 131088 | tf_op jit(solution)/shard_map/reduce_scatter | solution.py:203
  (130 shorter events, 10.5 us)
Async XLA Ops:
  7.2 6.5 copy-start
  7.2 236.7 %all-reduce.13.cloned.1.call-start = ((), (), s32[]{:S(2)}) async-start(), calls=%async_computation.3 | async-start | bytes 2097152 | tf_op jit(solution)/shard_map/psum | solution.py:56
  15.0 294.5 %all-gather.9.cloned.1.call-start = ((), (), s32[]{:S(2)}) async-start(), calls=%async_computation.8 | async-start | bytes 2162688 | tf_op jit(solution)/shard_map/all_gather | solution.py:43
  15.8 537.2 %all-reduce.17.cloned.1.call-start = ((), (), s32[]{:S(2)}) async-start(), calls=%async_computation.12 | async-start | bytes 4194304
  15.8 7.2 copy-start.29
  15.8 11.1 copy-start.8
  243.9 3.3 copy-start.4
  245.8 68.0 %copy-start.10 = (f32[256,8]{1,0:T(8,128)}, f32[256,8]{1,0:T(8,128)S(1)}, u32[]{:S(2)}) copy-start(f32[256,8]{1,0:T(8,128)S(1)} %add_rsqrt_fusion) | copy-start | bytes 24580
  246.2 1.0 copy-start.5
  313.8 3.4 copy-start.2
  317.3 6.0 copy-start.1
  321.1 1.1 copy-start.26
  322.1 3.3 copy-start.13
  323.3 2.9 copy-start.24
  323.3 3.6 copy-start.30
  323.3 229.6 %copy-start.15 = (bf16[4,8192]{1,0:T(4,128)(2,1)S(1)}, bf16[4,8192]{1,0:T(4,128)(2,1)}, u32[]{:S(2)}) copy-start(bf16[4,8192]{1,0:T(4,128)(2,1)} %param.11) | copy-start | bytes 196612
  325.5 293.4 %all-gather.13.cloned.1.call-start = ((), (), s32[]{:S(2)}) async-start(), calls=%async_computation.10 | async-start | bytes 2162688 | tf_op jit(solution)/shard_map/all_gather | solution.py:43
  326.9 358.6 %all-gather.11.cloned.1.call-start = ((), (), s32[]{:S(2)}) async-start(), calls=%async_computation.9 | async-start | bytes 2162688 | tf_op jit(solution)/shard_map/all_gather | solution.py:43
  553.9 143.1 %copy-start.20 = (bf16[4,8192]{1,0:T(4,128)(2,1)}, bf16[4,8192]{1,0:T(4,128)(2,1)S(1)}, u32[]{:S(2)}) copy-start(bf16[4,8192]{1,0:T(4,128)(2,1)S(1)} %add_convert_fusion.1) | copy-start | bytes 196612
  553.9 5.7 collective-permute-start
  559.6 0.6 copy-start.16
  560.2 372.6 %all-reduce.19.cloned.1.call-start = ((), (), s32[]{:S(2)}) async-start(), calls=%async_computation.13 | async-start | bytes 4194304
  689.9 3.4 copy-start.3
  693.3 4.9 copy-start.14
  697.0 3.5 copy-start.28
  697.0 8.6 copy-start.11
  700.5 5.2 copy-start.17
  700.5 233.5 %copy-start.25 = (bf16[4,8192]{1,0:T(4,128)(2,1)S(1)}, bf16[4,8192]{1,0:T(4,128)(2,1)}, u32[]{:S(2)}) copy-start(bf16[4,8192]{1,0:T(4,128)(2,1)} %param.18) | copy-start | bytes 196612
  700.5 241.9 %copy-start.27 = (bf16[128,2,128]{0,2,1:T(8,128)(2,1)S(1)}, bf16[128,2,128]{0,2,1:T(8,128)(2,1)}, u32[]{:S(2)}) copy-start(bf16[128,2,128]{0,2,1:T(8,128)(2,1)} %copy-done.26) | copy-start | bytes 196612
  705.6 298.8 %all-gather.15.cloned.1.call-start = ((), (), s32[]{:S(2)}) async-start(), calls=%async_computation.11 | async-start | bytes 2162688 | tf_op jit(solution)/shard_map/all_gather | solution.py:43
  935.0 77.8 %copy-start.22 = (bf16[4,8192]{1,0:T(4,128)(2,1)}, bf16[4,8192]{1,0:T(4,128)(2,1)S(1)}, u32[]{:S(2)}) copy-start(bf16[4,8192]{1,0:T(4,128)(2,1)S(1)} %fusion.69) | copy-start | bytes 196612
  935.0 6.5 collective-permute-start.1
  942.2 300.3 %all-reduce.15.cloned.1.call-start = ((), (), s32[]{:S(2)}) async-start(), calls=%async_computation.4 | async-start | bytes 2097152 | tf_op jit(solution)/shard_map/psum | solution.py:56
  1008.5 6.1 copy-start.19
  1018.3 250.0 %reduce-scatter.8.cloned.1.call-start = ((), (), s32[]{:S(2)}) async-start(), calls=%async_computation.7 | async-start | bytes 1310720 | tf_op jit(solution)/shard_map/reduce_scatter | solution.py:210
  1132.8 163.9 %reduce-scatter.6.cloned.1.call-start = ((), (), s32[]{:S(2)}) async-start(), calls=%async_computation.6 | async-start | bytes 1310720 | tf_op jit(solution)/shard_map/reduce_scatter | solution.py:209
  1242.5 3.5 copy-start.6
  1242.5 3.5 copy-start.7
  1248.1 5.6 copy-start.12
  1248.1 287.6 %all-reduce.21.cloned.1.call-start = ((), (), s32[]{:S(2)}) async-start(), calls=%async_computation.14 | async-start | bytes 8388608
  1260.3 1.1 copy-start.9
  1260.3 276.6 %copy-start.18 = (bf16[4,8192]{1,0:T(4,128)(2,1)S(1)}, bf16[4,8192]{1,0:T(4,128)(2,1)}, u32[]{:S(2)}) copy-start(bf16[4,8192]{1,0:T(4,128)(2,1)} %copy-done.16) | copy-start | bytes 196612
  1260.3 276.6 %copy-start.21 = (bf16[4,8192]{1,0:T(4,128)(2,1)S(1)}, bf16[4,8192]{1,0:T(4,128)(2,1)}, u32[]{:S(2)}) copy-start(bf16[4,8192]{1,0:T(4,128)(2,1)} %copy-done.20) | copy-start | bytes 196612
  1260.3 276.6 %copy-start.23 = (bf16[4,8192]{1,0:T(4,128)(2,1)S(1)}, bf16[4,8192]{1,0:T(4,128)(2,1)}, u32[]{:S(2)}) copy-start(bf16[4,8192]{1,0:T(4,128)(2,1)} %copy-done.22) | copy-start | bytes 196612
  1260.3 295.2 %reduce-scatter.4.cloned.1.call-start = ((), (), s32[]{:S(2)}) async-start(), calls=%async_computation.5 | async-start | bytes 393216 | tf_op jit(solution)/shard_map/reduce_scatter | solution.py:203
Sparse Core Ops, SparseCore 0:
  15.1 228.7 all-reduce.12
  245.9 63.5 all-gather.8
  325.6 227.2 all-reduce.16
  555.2 63.5 all-gather.12
  621.1 64.3 all-gather.10
  705.8 226.9 all-reduce.18
  942.4 62.0 all-gather.14
  1018.4 224.0 all-reduce.14
  1245.1 23.1 reduce-scatter.7
  1270.8 25.8 reduce-scatter.5
  1299.4 236.2 all-reduce.20
  1538.6 16.8 reduce-scatter.3
where the time goes:
time: 1560 us
  waiting for transfers between devices  1190 us (76%)
  blocking collectives  238 us (15%)
  matrix products  53.6 us (3%)
  local copies, waits for them, and re-layouts  35.6 us (2%)
  other arithmetic  22.3 us (1%)
  between operations  17.5 us (1%)
    unnamed x15, waiting for transfers between devices  690 us
    all_gather x4, waiting for transfers between devices, token_rows(): lax.all_gather(shard, 'tensor', axis=0, tiled=True)  235 us
    psum x2, blocking collectives, kv_totals(): return lax.psum((keys_part, values_part), 'tensor')  231 us
    psum x2, waiting for transfers between devices, kv_totals(): return lax.psum((keys_part, values_part), 'tensor')  208 us
  transfers between devices with their start and end apart: 14, of which 14 were waited for; matrix products, arithmetic and copies ran while one was open for 4% of the time, Pallas kernels for 0%

commit v1 on v0

--- a/solution.py
+++ b/solution.py
@@ -40,7 +40,16 @@
 
 
 def token_rows(shard, transform):
-    return transform(lax.all_gather(shard, "tensor", axis=0, tiled=True), jnp.int32(0))
+    connect_words_on_mesh = lambda local: jnp.concatenate(
+        lax.all_to_all(
+            jnp.stack([local for _ in range(lax.axis_size("tensor"))]),
+            axis_name="tensor",
+            split_axis=0,
+            concat_axis=0,
+        ),
+        axis=0,
+    )
+    return transform(connect_words_on_mesh(shard), jnp.int32(0))
 
 
 def token_sums(term, shard_rows):

time: 1560 us -> 1460 us (0.936)
  waiting for transfers between devices: 1190 us -> 1020 us
  starting transfers between devices: 6.54 us -> 35.3 us
  blocking collectives: 238 us -> 262 us
    all_gather x4 -> x0, waiting for transfers between devices: 235 us -> none  [token_rows(): lax.all_gather(shard, 'tensor', axis=0, tiled=True)]
    all_to_all x0 -> x4, waiting for transfers between devices: none -> 85.2 us  [token_rows(): lax.all_to_all(jnp.stack([local for _ in range(lax.axis_size('tensor'))])...]
    all_to_all x0 -> x4, starting transfers between devices: none -> 29 us  [token_rows(): lax.all_to_all(jnp.stack([local for _ in range(lax.axis_size('tensor'))])...]
    psum x2, waiting for transfers between devices: 208 us -> 182 us  [kv_totals(): return lax.psum((keys_part, values_part), 'tensor')]
    psum x2, blocking collectives: 231 us -> 255 us  [kv_totals(): return lax.psum((keys_part, values_part), 'tensor')]
    unnamed x15 -> x11, waiting for transfers between devices: 690 us -> 698 us
  transfers between devices with their start and end apart: 14 -> 14, of which waited for: 14 -> 12; matrix products, arithmetic and copies ran while one was open for 4% -> 5% of each run, Pallas kernels for 0% -> 0%
where the time goes in v1:
time: 1460 us; the launch traced here: 1450 us
  waiting for transfers between devices  1020 us (70%)
  blocking collectives  262 us (18%)
  matrix products  52.3 us (4%)
  local copies, waits for them, and re-layouts  43.2 us (3%)
  starting transfers between devices  35.3 us (2%)
  other arithmetic  20.9 us (1%)
  between operations  17.6 us (1%)
    unnamed x11, waiting for transfers between devices  698 us
    psum x2, blocking collectives, kv_totals(): return lax.psum((keys_part, values_part), 'tensor')  255 us
    psum x2, waiting for transfers between devices, kv_totals(): return lax.psum((keys_part, values_part), 'tensor')  182 us
    all_to_all x4, waiting for transfers between devices, token_rows(): lax.all_to_all(jnp.stack([local for _ in range(lax.axis_size('tensor'))])...  85.2 us
  transfers between devices with their start and end apart: 14, of which 12 were waited for; matrix products, arithmetic and copies ran while one was open for 5% of the time, Pallas kernels for 0%

profile of v1, /device:TPU:1, one launch (start us, length us, event | category | flops | bytes accessed | tf_op | source)
XLA Modules:
  0.0 1453.2 jit_solution(9643870707142028241)
XLA Ops:
  7.2 6.5 all_gather.3
  13.7 1.3 fusion.47
  15.0 2.3 stack.8
  17.3 11.6 all-to-all-start
  30.8 2.5 and_reduce_fusion
  33.4 6.5 copy.96
  40.6 1.3 fusion.50
  42.7 142.6 %all-reduce.22 = bf16[256,1024]{1,0:T(8,128)(2,1)} all-reduce(f32[256,1024]{1,0:T(8,128)} %fusion.50), channel_id=1, replica_groups=mesh['dp'=4,'depth'=2,'tensor'=32] {'tensor'}, use_global_device_ids=true, to_apply=%region_0.1 | all-reduce | flops 262144 | bytes 1572864 | tf_op jit(solution)/shard_map/psum | solution.py:65
  185.3 75.0 %all-reduce.13.cloned.1.call-done = f32[256,1024]{1,0:T(8,128)} async-done(((f32[256,1024]{1,0:T(8,128)}), f32[256,1024]{1,0:T(8,128)}) %all-reduce.13.cloned.1.call-update) | async-done | bytes 1048592 | tf_op jit(solution)/shard_map/psum | solution.py:65
  260.3 1.5 copy.99
  266.1 2.3 stack.10
  268.4 5.9 all-to-all-start.2
  274.4 1.2 fusion.2
  275.6 2.5 fusion.3
  278.1 2.5 reshape.280
  280.6 3.6 multiply_reduce_fusion.8
  284.3 1.1 fusion.101
  287.2 2.1 convolution_convert_fusion.3
  291.2 234.1 %all-reduce.17.cloned.1.call-done = bf16[128,8192]{1,0:T(8,128)(2,1)} async-done(((bf16[128,8192]{1,0:T(8,128)(2,1)}), bf16[128,8192]{1,0:T(8,128)(2,1)}) %all-reduce.17.cloned.1.call-update) | async-done | bytes 2097168
  526.3 4.5 collective-permute-start
  530.8 1.1 collective-permute-done
  531.9 2.3 stack.9
  534.2 5.3 all-to-all-start.1
  539.6 4.0 reshape.273
  543.6 4.4 fusion.39
  548.6 1.7 convolution_bitcast_fusion.3
  550.3 38.7 %all-to-all-done.1 = bf16[32,4,8192]{2,1,0:T(4,128)(2,1)S(1)} async-done(((bf16[32,4,8192]{2,1,0:T(4,128)(2,1)}), bf16[32,4,8192]{2,1,0:T(4,128)(2,1)S(1)}, u32[]{:S(2)}, u32[]{:S(2)}) %all-to-all-start.1) | async-done | bytes 2097184 | tf_op jit(solution)/shard_map/all_to_all | solution.py:44
  589.0 1.2 fusion.4
  590.2 2.4 fusion.5
  592.6 2.5 reshape.283
  595.1 3.5 multiply_reduce_fusion.7
  598.7 1.1 fusion.102
  599.9 1.4 multiply_reduce_fusion.5
  601.4 5.0 convolution_convert_fusion.1
  607.5 226.9 %all-reduce.19.cloned.1.call-done = bf16[128,8192]{1,0:T(8,128)(2,1)} async-done(((bf16[128,8192]{1,0:T(8,128)(2,1)}), bf16[128,8192]{1,0:T(8,128)(2,1)}) %all-reduce.19.cloned.1.call-update) | async-done | bytes 2097168
  834.4 1.2 fusion.67
  835.5 1.0 fusion.65
  836.6 1.3 collective-permute-start.1
  837.9 5.2 collective-permute-done.1
  843.7 2.3 stack.11
  846.0 6.1 all-to-all-start.3
  852.3 1.9 convolution_bitcast_fusion.6
  855.0 46.6 %all-to-all-done.3 = bf16[32,4,8192]{2,1,0:T(4,128)(2,1)} async-done(((bf16[32,4,8192]{2,1,0:T(4,128)(2,1)}), bf16[32,4,8192]{2,1,0:T(4,128)(2,1)}, u32[]{:S(2)}, u32[]{:S(2)}) %all-to-all-start.3) | async-done | bytes 2097184 | tf_op jit(solution)/shard_map/all_to_all | solution.py:44
  901.6 2.5 reshape.276
  904.1 3.8 fusion.36
  909.1 1.3 fusion.34
  910.6 1.5 bitcast_multiply_fusion
  912.1 112.6 %all-reduce.23 = bf16[256,1024]{1,0:T(8,128)(2,1)S(1)} all-reduce(f32[256,1024]{1,0:T(8,128)S(1)} %get-tuple-element.29), channel_id=1, replica_groups=mesh['dp'=4,'depth'=2,'tensor'=32] {'tensor'}, use_global_device_ids=true, to_apply=%region_24.25 | all-reduce | flops 262144 | bytes 1572864 | tf_op jit(solution)/shard_map/psum | solution.py:65
  1024.7 1.4 convolution_bitcast_fusion
  1026.4 106.9 %all-reduce.15.cloned.1.call-done = f32[256,1024]{1,0:T(8,128)} async-done(((f32[256,1024]{1,0:T(8,128)}), f32[256,1024]{1,0:T(8,128)}) %all-reduce.15.cloned.1.call-update) | async-done | bytes 1048592 | tf_op jit(solution)/shard_map/psum | solution.py:65
  1133.3 1.4 copy.102
  1137.4 1.3 convolution_bitcast_fusion.1
  1139.8 4.3 convolution_convert_fusion.2
  1144.1 1.3 multiply_reduce_fusion.4
  1145.5 5.1 convolution_convert_fusion
  1151.0 1.1 convolution_add_fusion
  1152.1 6.9 reduce-scatter.8.cloned.1.call-done
  1158.9 1.8 copy.79
  1160.7 26.7 %reduce-scatter.6.cloned.1.call-done = f32[256,256]{0,1:T(8,128)} async-done(((f32[256,1024]{0,1:T(8,128)}), f32[256,256]{0,1:T(8,128)}) %reduce-scatter.6.cloned.1.call-update) | async-done | bytes 262160 | tf_op jit(solution)/shard_map/reduce_scatter | solution.py:218
  1187.4 1.8 copy.78
  1189.2 237.3 %all-reduce.21.cloned.1.call-done = (bf16[128,8192]{1,0:T(8,128)(2,1)}, bf16[128,8192]{1,0:T(8,128)(2,1)}) async-done(((bf16[128,8192]{1,0:T(8,128)(2,1)}, bf16[128,8192]{1,0:T(8,128)(2,1)}), (bf16[128,8192]{1,0:T(8,128)(2,1)}, bf16[128,8192]{1,0:T(8,128)(2,1)})) %all-reduce.21.cloned.1.call-update) | async-done | bytes 4194320
  1426.4 1.2 fusion.71
  1427.6 1.8 fusion.80
  1429.5 16.9 %reduce-scatter.4.cloned.1.call-done = f32[128,256]{1,0:T(8,128)} async-done(((f32[256,256]{1,0:T(8,128)}), f32[128,256]{1,0:T(8,128)}) %reduce-scatter.4.cloned.1.call-update) | async-done | bytes 131088 | tf_op jit(solution)/shard_map/reduce_scatter | solution.py:212
  (156 shorter events, 19.1 us)
Async XLA Ops:
  7.2 6.5 copy-start
  7.2 7.9 copy-start.20
  7.2 253.1 %all-reduce.13.cloned.1.call-start = ((), (), s32[]{:S(2)}) async-start(), calls=%async_computation.7 | async-start | bytes 2097152 | tf_op jit(solution)/shard_map/psum | solution.py:65
  17.3 12.3 copy-start.41
  17.3 248.8 %all-to-all-start = ((bf16[32,4,8192]{2,1,0:T(4,128)(2,1)}), bf16[32,4,8192]{2,1,0:T(4,128)(2,1)S(1)}, u32[]{:S(2)}, u32[]{:S(2)}) async-start(bf16[32,4,8192]{2,1,0:T(4,128)(2,1)} %stack.8), calls=%async_computation | async-start | bytes 4194304 | tf_op jit(solution)/shard_map/all_to_all | solution.py:44
  33.3 7.3 copy-start.9
  33.3 9.3 copy-start.34
  260.3 4.9 copy-start.4
  261.8 1.0 copy-start.2
  263.1 0.7 copy-start.12
  264.1 1.0 copy-start.6
  268.4 262.4 %all-to-all-start.2 = ((bf16[32,4,8192]{2,1,0:T(4,128)(2,1)}), bf16[32,4,8192]{2,1,0:T(4,128)(2,1)}, u32[]{:S(2)}, u32[]{:S(2)}) async-start(bf16[32,4,8192]{2,1,0:T(4,128)(2,1)} %stack.10), calls=%async_computation.2 | async-start | bytes 4194304 | tf_op jit(solution)/shard_map/all_to_all | solution.py:44
  274.4 250.9 %all-reduce.17.cloned.1.call-start = ((), (), s32[]{:S(2)}) async-start(), calls=%async_computation.12 | async-start | bytes 4194304
  280.6 3.7 copy-start.39
  280.6 6.5 copy-start.1
  284.3 1.1 copy-start.36
  285.4 0.7 copy-start.16
  289.3 0.7 copy-start.42
  289.3 236.0 %copy-start.21 = (bf16[4,8192]{1,0:T(4,128)(2,1)S(1)}, bf16[4,8192]{1,0:T(4,128)(2,1)}, u32[]{:S(2)}) copy-start(bf16[4,8192]{1,0:T(4,128)(2,1)} %param.11) | copy-start | bytes 196612
  526.3 8.0 copy-start.28
  526.3 5.7 collective-permute-start
  531.9 2.3 copy-start.23
  534.2 54.7 %all-to-all-start.1 = ((bf16[32,4,8192]{2,1,0:T(4,128)(2,1)}), bf16[32,4,8192]{2,1,0:T(4,128)(2,1)S(1)}, u32[]{:S(2)}, u32[]{:S(2)}) async-start(bf16[32,4,8192]{2,1,0:T(4,128)(2,1)} %stack.9), calls=%async_computation.1 | async-start | bytes 4194304 | tf_op jit(solution)/shard_map/all_to_all | solution.py:44
  539.6 294.8 %all-reduce.19.cloned.1.call-start = ((), (), s32[]{:S(2)}) async-start(), calls=%async_computation.13 | async-start | bytes 4194304
  548.0 0.6 copy-start.18
  595.1 3.6 copy-start.40
  595.1 4.7 copy-start.17
  598.7 7.7 copy-start.14
  598.7 253.5 %copy-start.38 = (bf16[128,2,128]{0,2,1:T(8,128)(2,1)}, bf16[128,2,128]{0,2,1:T(8,128)(2,1)S(1)}, u32[]{:S(2)}) copy-start(bf16[128,2,128]{0,2,1:T(8,128)(2,1)S(1)} %get-tuple-element.28) | copy-start | bytes 196612
  599.9 252.3 %copy-start.27 = (f32[2,128,256]{1,2,0:T(8,128)}, f32[2,128,256]{1,2,0:T(8,128)S(1)}, u32[]{:S(2)}) copy-start(f32[2,128,256]{1,2,0:T(8,128)S(1)} %get-tuple-element.26) | copy-start | bytes 786436
  606.4 0.8 copy-start.22
  606.4 0.9 copy-start.24
  606.4 229.1 %copy-start.35 = (bf16[4,8192]{1,0:T(4,128)(2,1)S(1)}, bf16[4,8192]{1,0:T(4,128)(2,1)}, u32[]{:S(2)}) copy-start(bf16[4,8192]{1,0:T(4,128)(2,1)} %param.18) | copy-start | bytes 196612
  607.5 238.5 %copy-start.10 = (bf16[4,8192]{1,0:T(4,128)(2,1)}, bf16[4,8192]{1,0:T(4,128)(2,1)S(1)}, u32[]{:S(2)}) copy-start(bf16[4,8192]{1,0:T(4,128)(2,1)S(1)} %get-tuple-element.25) | copy-start | bytes 196612
  836.6 1.3 copy-start.32
  836.6 6.5 collective-permute-start.1
  843.1 0.6 copy-start.30
  846.0 6.3 copy-start.37
  846.0 8.2 copy-start.19
  846.0 55.6 %all-to-all-start.3 = ((bf16[32,4,8192]{2,1,0:T(4,128)(2,1)}), bf16[32,4,8192]{2,1,0:T(4,128)(2,1)}, u32[]{:S(2)}, u32[]{:S(2)}) async-start(bf16[32,4,8192]{2,1,0:T(4,128)(2,1)} %stack.11), calls=%async_computation.3 | async-start | bytes 4194304 | tf_op jit(solution)/shard_map/all_to_all | solution.py:44
  852.1 281.2 %all-reduce.15.cloned.1.call-start = ((), (), s32[]{:S(2)}) async-start(), calls=%async_computation.8 | async-start | bytes 2097152 | tf_op jit(solution)/shard_map/psum | solution.py:65
  904.1 4.8 copy-start.26
  912.1 246.9 %reduce-scatter.8.cloned.1.call-start = ((), (), s32[]{:S(2)}) async-start(), calls=%async_computation.11 | async-start | bytes 1310720 | tf_op jit(solution)/shard_map/reduce_scatter | solution.py:219
  1024.7 110.1 %copy-start.3 = (f32[32,8,8,128]{3,2,1,0:T(8,128)S(1)}, f32[32,8,8,128]{3,2,1,0:T(8,128)}, u32[]{:S(2)}) copy-start(f32[32,8,8,128]{3,2,1,0:T(8,128)} %copy-done.2) | copy-start | bytes 3145732
  1024.7 110.1 %copy-start.13 = (f32[256,8]{1,0:T(8,128)S(1)}, f32[256,8]{1,0:T(8,128)}, u32[]{:S(2)}) copy-start(f32[256,8]{1,0:T(8,128)} %copy-done.12) | copy-start | bytes 24580
  1026.1 161.2 %reduce-scatter.6.cloned.1.call-start = ((), (), s32[]{:S(2)}) async-start(), calls=%async_computation.10 | async-start | bytes 1310720 | tf_op jit(solution)/shard_map/reduce_scatter | solution.py:218
  1134.8 1.2 copy-start.5
  1134.8 1.5 copy-start.7
  1134.8 1.8 copy-start.8
  1138.7 287.7 %all-reduce.21.cloned.1.call-start = ((), (), s32[]{:S(2)}) async-start(), calls=%async_computation.14 | async-start | bytes 8388608
  1139.8 4.3 copy-start.15
  1150.5 275.9 %copy-start.11 = (bf16[4,8192]{1,0:T(4,128)(2,1)S(1)}, bf16[4,8192]{1,0:T(4,128)(2,1)}, u32[]{:S(2)}) copy-start(bf16[4,8192]{1,0:T(4,128)(2,1)} %copy-done.10) | copy-start | bytes 196612
  1150.6 277.1 %copy-start.25 = (bf16[4,8192]{1,0:T(4,128)(2,1)S(1)}, bf16[4,8192]{1,0:T(4,128)(2,1)}, u32[]{:S(2)}) copy-start(bf16[4,8192]{1,0:T(4,128)(2,1)} %copy-done.23) | copy-start | bytes 196612
  1150.6 277.0 %copy-start.29 = (bf16[4,8192]{1,0:T(4,128)(2,1)S(1)}, bf16[4,8192]{1,0:T(4,128)(2,1)}, u32[]{:S(2)}) copy-start(bf16[4,8192]{1,0:T(4,128)(2,1)} %copy-done.28) | copy-start | bytes 196612
  1150.6 277.0 %copy-start.31 = (bf16[4,8192]{1,0:T(4,128)(2,1)S(1)}, bf16[4,8192]{1,0:T(4,128)(2,1)}, u32[]{:S(2)}) copy-start(bf16[4,8192]{1,0:T(4,128)(2,1)} %copy-done.30) | copy-start | bytes 196612
  1150.6 277.0 %copy-start.33 = (bf16[4,8192]{1,0:T(4,128)(2,1)S(1)}, bf16[4,8192]{1,0:T(4,128)(2,1)}, u32[]{:S(2)}) copy-start(bf16[4,8192]{1,0:T(4,128)(2,1)} %copy-done.32) | copy-start | bytes 196612
  1150.6 295.8 %reduce-scatter.4.cloned.1.call-start = ((), (), s32[]{:S(2)}) async-start(), calls=%async_computation.9 | async-start | bytes 393216 | tf_op jit(solution)/shard_map/reduce_scatter | solution.py:212
Sparse Core Ops, SparseCore 0:
  15.2 245.0 all-reduce.12
  289.4 235.8 all-reduce.16
  606.6 227.7 all-reduce.18
  912.2 221.1 all-reduce.14
  1135.7 23.1 reduce-scatter.7
  1161.5 25.8 reduce-scatter.5
  1190.1 236.3 all-reduce.20
  1429.5 16.8 reduce-scatter.3
